TPU v7x, 256 devices: a whole 4x4x8 slice. The times are simulated.
256 devices in a mesh: aper: 64 (over z_hi, y, x), shot: 4 (over z_lo, core).
Axes of the slice: x: 4, y: 4, z: 8 (z_hi: 4, z_lo: 2; z = z_hi * 2 + z_lo), core: 2. Of those that a mesh axis runs over, the one named last changes fastest.
Arguments:
- wavefield: float32 [4, 9, 256, 128, 128], P('shot', None, 'aper'), may hold values from -6 to 6
- lame_lambda: float32 [256, 128, 128], P('aper', 'shot'), may hold values from 0.5 to 2
- lame_mu: float32 [256, 128, 128], P('aper', 'shot'), may hold values from 0.3 to 1
- buoyancy: float32 [256, 128, 128], P('aper', 'shot'), may hold values from 0.4 to 1
- quality: float32 [256, 128, 128], P('aper', 'shot'), may hold values from 0.05 to 2
- active: int32 [4, 64, 4, 4], replicated, may hold values 0 or 1
Outputs:
- final_field: float32 [4, 9, 256, 128, 128], P('shot', None, 'aper')
All inputs are finite; a program needn't handle non-finite values.
Results may differ from a plain program's by a relative error of at most 0.00002.
Values sent between devices are 32-bit elements; how exact they have to be, the bound alone decides.
A program may use at most 64 MiB of HBM per device.

v0:
```python
import jax
import jax.numpy as jnp
from jax import lax
from jax.sharding import PartitionSpec as P

BLK = 32
STEPS = 4
COEF_NEAR = 1.125
COEF_FAR = -1.0 / 24.0
TIME_STEP = 0.2


def extended(shard, sides, width):
    for axis, dim in sides:
        devices, length = (lax.axis_size(axis), shard.shape[dim])
        up = [(i, (i + 1) % devices) for i in range(devices - 1)]
        down = [(j, i) for i, j in up]
        last = lax.slice_in_dim(shard, length - width, length, axis=dim)
        initial = lax.slice_in_dim(shard, 0, width, axis=dim)
        before = lax.ppermute(last, axis, up)
        after = lax.ppermute(initial, axis, down)
        shard = jnp.concatenate([before, shard, after], axis=dim)
    return shard


def forward_rows(values, offset, length):
    return COEF_NEAR * (
        values[offset + 1 : offset + 1 + length] - values[offset : offset + length]
    ) + COEF_FAR * (
        values[offset + 2 : offset + 2 + length] - values[offset - 1 : offset - 1 + length]
    )


def backward_rows(values, offset, length):
    return COEF_NEAR * (
        values[offset : offset + length] - values[offset - 1 : offset - 1 + length]
    ) + COEF_FAR * (
        values[offset + 1 : offset + 1 + length] - values[offset - 2 : offset - 2 + length]
    )


def shifted(values, along, amount):
    widths = [(0, 0)] * values.ndim
    widths[along] = (2, 2)
    padded = jnp.pad(values, widths)
    return lax.slice_in_dim(padded, 2 + amount, 2 + amount + values.shape[along], axis=along)


def forward_axis(values, along):
    return COEF_NEAR * (shifted(values, along, 1) - values) + COEF_FAR * (
        shifted(values, along, 2) - shifted(values, along, -1)
    )


def backward_axis(values, along):
    return COEF_NEAR * (values - shifted(values, along, -1)) + COEF_FAR * (
        shifted(values, along, 1) - shifted(values, along, -2)
    )


def velocity_update(previous, stress, offset, length, buoyancy, damping, active_cells):

    def pick_rows(values):
        return values[offset : offset + length]

    grad_first = (
        forward_rows(stress[0], offset, length)
        + backward_axis(pick_rows(stress[3]), 1)
        + backward_axis(pick_rows(stress[4]), 2)
    )
    grad_second = (
        backward_rows(stress[3], offset, length)
        + forward_axis(pick_rows(stress[1]), 1)
        + backward_axis(pick_rows(stress[5]), 2)
    )
    grad_third = (
        backward_rows(stress[4], offset, length)
        + backward_axis(pick_rows(stress[5]), 1)
        + forward_axis(pick_rows(stress[2]), 2)
    )
    forcing = jnp.stack([grad_first, grad_second, grad_third])
    return previous + active_cells * (
        damping * (previous + TIME_STEP * buoyancy * forcing) - previous
    )


def stress_update(previous, velocity, offset, length, lambda_field, shear, damping, active_cells):

    def pick_rows(values):
        return values[offset : offset + length]

    strain_first = backward_rows(velocity[0], offset, length)
    strain_second = backward_axis(pick_rows(velocity[1]), 1)
    strain_third = backward_axis(pick_rows(velocity[2]), 2)
    dilation = strain_first + strain_second + strain_third
    shear_xy = forward_axis(pick_rows(velocity[0]), 1) + forward_rows(velocity[1], offset, length)
    shear_xz = forward_axis(pick_rows(velocity[0]), 2) + forward_rows(velocity[2], offset, length)
    shear_yz = forward_axis(pick_rows(velocity[1]), 2) + forward_axis(pick_rows(velocity[2]), 1)
    rates = jnp.stack(
        [
            lambda_field * dilation + 2.0 * shear * strain_first,
            lambda_field * dilation + 2.0 * shear * strain_second,
            lambda_field * dilation + 2.0 * shear * strain_third,
            shear * shear_xy,
            shear * shear_xz,
            shear * shear_yz,
        ]
    )
    return previous + active_cells * (damping * (previous + TIME_STEP * rates) - previous)


def upsample(blocks):
    return jnp.repeat(jnp.repeat(blocks, BLK, axis=1), BLK, axis=2)


def per_device(wavefield, lame_lambda, lame_mu, buoyancy, quality, active):
    panels = (
        lax.all_gather(lame_lambda, "shot", axis=1, tiled=True),
        lax.all_gather(lame_mu, "shot", axis=1, tiled=True),
        lax.all_gather(buoyancy, "shot", axis=1, tiled=True),
        lax.all_gather(quality, "shot", axis=1, tiled=True),
    )
    model = jnp.stack(panels)
    values = wavefield[0]
    slab_rows = values.shape[1]
    device = lax.axis_index("aper")
    damping = jnp.exp(-TIME_STEP * model[3])
    for moment in range(STEPS):
        blocks = lax.dynamic_index_in_dim(
            active[moment].astype(jnp.float32), device, 0, keepdims=True
        )
        active_cells = upsample(blocks)
        stress_pad = extended(values[3:], (("aper", 1),), 2)
        velocity = velocity_update(
            values[:3], stress_pad, 2, slab_rows, model[2], damping, active_cells
        )
        velocity_pad = extended(velocity, (("aper", 1),), 2)
        stress = stress_update(
            values[3:], velocity_pad, 2, slab_rows, model[0], model[1], damping, active_cells
        )
        values = jnp.concatenate([velocity, stress], axis=0)
    return values[None]


def solution(mesh):
    return jax.shard_map(
        per_device,
        mesh=mesh,
        in_specs=(
            P("shot", None, "aper", None, None),
            P("aper", "shot", None),
            P("aper", "shot", None),
            P("aper", "shot", None),
            P("aper", "shot", None),
            P(),
        ),
        out_specs=P("shot", None, "aper", None, None),
        check_vma=False,
    )
```

profile of v0, /device:TPU:126, one launch (start us, length us, event | category | flops | bytes accessed | tf_op | source)
XLA Modules:
  0.0 352.6 jit_solution(15949601193661434074)
XLA Ops:
  0.0 1.5 slice_bitcast_fusion
  1.5 1.2 fusion.436
  2.8 2.7 collective-permute-start
  5.5 9.4 %collective-permute-start.1 = (f32[6,2,128,128]{3,2,1,0:T(8,128)}, f32[6,2,128,128]{3,2,1,0:T(8,128)}, u32[]{:S(2)}, u32[]{:S(2)}) collective-permute-start(f32[6,2,128,128]{3,2,1,0:T(8,128)} %get-tuple-element.48), channel_id=1, source_target_pairs={{0,4},{4,8},{8,12},{12,16},{16,20},{20,24},{24,28},{28,32},{32,36}... | collective-permute-start | bytes 2359304 | tf_op jit(solution)/shard_map/ppermute | solution.py:20
  15.0 0.6 fusion.441
  15.6 35.7 %all_gather.12 = f32[4,128,128]{2,1,0:T(8,128)S(1)} all-gather(f32[4,32,128]{2,1,0:T(8,128)S(1)} %copy-done.41), channel_id=1, replica_groups=mesh['aper'=64,'shot'=4] {'shot'}, dimensions={1}, use_global_device_ids=true | all-gather | bytes 327680 | tf_op jit(solution)/shard_map/all_gather | solution.py:121
  51.4 5.8 %all_gather.13 = f32[4,128,128]{2,1,0:T(8,128)S(1)} all-gather(f32[4,32,128]{2,1,0:T(8,128)S(1)} %copy-done.42), channel_id=1, replica_groups=mesh['aper'=64,'shot'=4] {'shot'}, dimensions={1}, use_global_device_ids=true | all-gather | bytes 327680 | tf_op jit(solution)/shard_map/all_gather | solution.py:120
  57.7 1.6 slice_bitcast_fusion.32
  59.3 0.6 copy-done
  59.9 1.3 fusion.31
  61.2 1.3 fusion.38
  62.5 1.2 fusion.24
  64.0 0.4 copy-done.15
  64.4 1.9 collective-permute-start.2
  66.3 3.9 %collective-permute-start.3 = (f32[3,2,128,128]{3,2,1,0:T(8,128)S(1)}, f32[3,2,128,128]{3,2,1,0:T(8,128)S(1)}, u32[]{:S(2)}, u32[]{:S(2)}) collective-permute-start(f32[3,2,128,128]{3,2,1,0:T(8,128)S(1)} %get-tuple-element.68), channel_id=1, source_target_pairs={{4,0},{8,4},{12,8},{16,12},{20,16},{24,20},{28,24},{32,28},{36,32}... | collective-permute-start | bytes 1179656 | tf_op jit(solution)/shard_map/ppermute | solution.py:21
  70.3 15.9 %all_gather.15 = f32[4,128,128]{2,1,0:T(8,128)S(1)} all-gather(f32[4,32,128]{2,1,0:T(8,128)S(1)} %copy-done.43), channel_id=1, replica_groups=mesh['aper'=64,'shot'=4] {'shot'}, dimensions={1}, use_global_device_ids=true | all-gather | bytes 327680 | tf_op jit(solution)/shard_map/all_gather | solution.py:119
  86.2 5.8 %all_gather.14 = f32[4,128,128]{2,1,0:T(8,128)S(1)} all-gather(f32[4,32,128]{2,1,0:T(8,128)S(1)} %copy-done.44), channel_id=1, replica_groups=mesh['aper'=64,'shot'=4] {'shot'}, dimensions={1}, use_global_device_ids=true | all-gather | bytes 327680 | tf_op jit(solution)/shard_map/all_gather | solution.py:118
  92.4 0.4 copy-done.19
  94.0 1.2 fusion.435
  95.2 1.9 collective-permute-start.4
  97.1 12.7 %collective-permute-start.5 = (f32[6,2,128,128]{3,2,1,0:T(8,128)}, f32[6,2,128,128]{3,2,1,0:T(8,128)}, u32[]{:S(2)}, u32[]{:S(2)}) collective-permute-start(f32[6,2,128,128]{3,2,1,0:T(8,128)} %get-tuple-element.46), channel_id=1, source_target_pairs={{0,4},{4,8},{8,12},{12,16},{16,20},{20,24},{24,28},{28,32},{32,36}... | collective-permute-start | bytes 2359304 | tf_op jit(solution)/shard_map/ppermute | solution.py:20
  110.1 0.6 broadcast_in_dim.61
  110.8 0.9 copy.10
  111.8 30.2 %collective-permute-done.4 = f32[6,2,128,128]{3,2,1,0:T(8,128)S(1)} collective-permute-done((f32[6,2,128,128]{3,2,1,0:T(8,128)}, f32[6,2,128,128]{3,2,1,0:T(8,128)S(1)}, u32[]{:S(2)}, u32[]{:S(2)}) %collective-permute-start.4) | collective-permute-done | bytes 786464 | tf_op jit(solution)/shard_map/ppermute | solution.py:21
  142.0 2.3 collective-permute-done.5
  144.4 1.3 fusion.75
  145.6 1.3 fusion.82
  147.0 1.2 fusion.68
  148.3 1.6 fusion.9
  150.0 10.7 %collective-permute-start.6 = (f32[3,2,128,128]{3,2,1,0:T(8,128)S(1)}, f32[3,2,128,128]{3,2,1,0:T(8,128)S(1)}, u32[]{:S(2)}, u32[]{:S(2)}) collective-permute-start(f32[3,2,128,128]{3,2,1,0:T(8,128)S(1)} %get-tuple-element.62), channel_id=1, source_target_pairs={{0,4},{4,8},{8,12},{12,16},{16,20},{20,24},{24,28},{28,32},{32,36}... | collective-permute-start | bytes 1179656 | tf_op jit(solution)/shard_map/ppermute | solution.py:20
  160.7 1.9 collective-permute-start.7
  162.7 10.9 %collective-permute-done.6 = f32[3,2,128,128]{3,2,1,0:T(8,128)S(1)} collective-permute-done((f32[3,2,128,128]{3,2,1,0:T(8,128)S(1)}, f32[3,2,128,128]{3,2,1,0:T(8,128)S(1)}, u32[]{:S(2)}, u32[]{:S(2)}) %collective-permute-start.6) | collective-permute-done | bytes 393248 | tf_op jit(solution)/shard_map/ppermute | solution.py:20
  173.5 9.0 %collective-permute-done.7 = f32[3,2,128,128]{3,2,1,0:T(8,128)S(1)} collective-permute-done((f32[3,2,128,128]{3,2,1,0:T(8,128)S(1)}, f32[3,2,128,128]{3,2,1,0:T(8,128)S(1)}, u32[]{:S(2)}, u32[]{:S(2)}) %collective-permute-start.7) | collective-permute-done | bytes 393248 | tf_op jit(solution)/shard_map/ppermute | solution.py:21
  183.6 0.4 copy-done.2
  184.4 1.3 fusion.434
  185.7 1.9 collective-permute-start.8
  187.6 10.2 %collective-permute-start.9 = (f32[6,2,128,128]{3,2,1,0:T(8,128)}, f32[6,2,128,128]{3,2,1,0:T(8,128)S(1)}, u32[]{:S(2)}, u32[]{:S(2)}) collective-permute-start(f32[6,2,128,128]{3,2,1,0:T(8,128)} %get-tuple-element.39), channel_id=1, source_target_pairs={{0,4},{4,8},{8,12},{12,16},{16,20},{20,24},{24,28},{28,32},{32,36}... | collective-permute-start | bytes 2359304 | tf_op jit(solution)/shard_map/ppermute | solution.py:20
  197.9 0.7 copy.21
  198.6 0.8 broadcast_in_dim.63
  199.4 0.7 broadcast_in_dim.64
  200.0 1.3 broadcast_in_dim.65
  201.3 1.6 copy.13
  203.0 25.6 %collective-permute-done.8 = f32[6,2,128,128]{3,2,1,0:T(8,128)S(1)} collective-permute-done((f32[6,2,128,128]{3,2,1,0:T(8,128)}, f32[6,2,128,128]{3,2,1,0:T(8,128)S(1)}, u32[]{:S(2)}, u32[]{:S(2)}) %collective-permute-start.8) | collective-permute-done | bytes 786464 | tf_op jit(solution)/shard_map/ppermute | solution.py:21
  228.6 1.3 collective-permute-done.9
  232.1 1.7 fusion.14
  233.9 10.7 %collective-permute-start.10 = (f32[3,2,128,128]{3,2,1,0:T(8,128)S(1)}, f32[3,2,128,128]{3,2,1,0:T(8,128)S(1)}, u32[]{:S(2)}, u32[]{:S(2)}) collective-permute-start(f32[3,2,128,128]{3,2,1,0:T(8,128)S(1)} %get-tuple-element.57), channel_id=1, source_target_pairs={{0,4},{4,8},{8,12},{12,16},{16,20},{20,24},{24,28},{28,32},{32,36}... | collective-permute-start | bytes 1179656 | tf_op jit(solution)/shard_map/ppermute | solution.py:20
  244.6 2.1 collective-permute-start.11
  246.8 8.4 %collective-permute-done.10 = f32[3,2,128,128]{3,2,1,0:T(8,128)S(1)} collective-permute-done((f32[3,2,128,128]{3,2,1,0:T(8,128)S(1)}, f32[3,2,128,128]{3,2,1,0:T(8,128)S(1)}, u32[]{:S(2)}, u32[]{:S(2)}) %collective-permute-start.10) | collective-permute-done | bytes 393248 | tf_op jit(solution)/shard_map/ppermute | solution.py:20
  255.2 16.0 %collective-permute-done.11 = f32[3,2,128,128]{3,2,1,0:T(8,128)S(1)} collective-permute-done((f32[3,2,128,128]{3,2,1,0:T(8,128)S(1)}, f32[3,2,128,128]{3,2,1,0:T(8,128)S(1)}, u32[]{:S(2)}, u32[]{:S(2)}) %collective-permute-start.11) | collective-permute-done | bytes 393248 | tf_op jit(solution)/shard_map/ppermute | solution.py:21
  272.7 1.3 fusion.433
  274.0 1.9 collective-permute-start.12
  275.9 10.2 %collective-permute-start.13 = (f32[6,2,128,128]{3,2,1,0:T(8,128)}, f32[6,2,128,128]{3,2,1,0:T(8,128)S(1)}, u32[]{:S(2)}, u32[]{:S(2)}) collective-permute-start(f32[6,2,128,128]{3,2,1,0:T(8,128)} %get-tuple-element.32), channel_id=1, source_target_pairs={{0,4},{4,8},{8,12},{12,16},{16,20},{20,24},{24,28},{28,32},{32,36}... | collective-permute-start | bytes 2359304 | tf_op jit(solution)/shard_map/ppermute | solution.py:20
  286.2 0.7 copy.22
  286.9 0.7 broadcast_in_dim.67
  287.7 0.6 broadcast_in_dim.69
  288.3 1.6 copy.16
  290.0 25.6 %collective-permute-done.12 = f32[6,2,128,128]{3,2,1,0:T(8,128)S(1)} collective-permute-done((f32[6,2,128,128]{3,2,1,0:T(8,128)}, f32[6,2,128,128]{3,2,1,0:T(8,128)S(1)}, u32[]{:S(2)}, u32[]{:S(2)}) %collective-permute-start.12) | collective-permute-done | bytes 786464 | tf_op jit(solution)/shard_map/ppermute | solution.py:21
  316.8 0.5 copy-done.4
  318.1 1.8 fusion.19
  320.0 10.6 %collective-permute-start.14 = (f32[3,2,128,128]{3,2,1,0:T(8,128)S(1)}, f32[3,2,128,128]{3,2,1,0:T(8,128)S(1)}, u32[]{:S(2)}, u32[]{:S(2)}) collective-permute-start(f32[3,2,128,128]{3,2,1,0:T(8,128)S(1)} %get-tuple-element.52), channel_id=1, source_target_pairs={{0,4},{4,8},{8,12},{12,16},{16,20},{20,24},{24,28},{28,32},{32,36}... | collective-permute-start | bytes 1179656 | tf_op jit(solution)/shard_map/ppermute | solution.py:20
  330.6 1.9 collective-permute-start.15
  332.6 6.5 %collective-permute-done.14 = f32[3,2,128,128]{3,2,1,0:T(8,128)S(1)} collective-permute-done((f32[3,2,128,128]{3,2,1,0:T(8,128)S(1)}, f32[3,2,128,128]{3,2,1,0:T(8,128)S(1)}, u32[]{:S(2)}, u32[]{:S(2)}) %collective-permute-start.14) | collective-permute-done | bytes 393248 | tf_op jit(solution)/shard_map/ppermute | solution.py:20
  339.1 10.4 %collective-permute-done.15 = f32[3,2,128,128]{3,2,1,0:T(8,128)S(1)} collective-permute-done((f32[3,2,128,128]{3,2,1,0:T(8,128)S(1)}, f32[3,2,128,128]{3,2,1,0:T(8,128)S(1)}, u32[]{:S(2)}, u32[]{:S(2)}) %collective-permute-start.15) | collective-permute-done | bytes 393248 | tf_op jit(solution)/shard_map/ppermute | solution.py:21
  351.0 1.6 maximum_bitcast_fusion
  (155 shorter events, 11.7 us)
Async XLA Ops:
  1.5 13.5 %copy-start.45 = (s32[4,64,4,4]{1,3,2,0:T(4,128)S(1)}, s32[4,64,4,4]{1,3,2,0:T(4,128)}, u32[]{:S(2)}) copy-start(s32[4,64,4,4]{1,3,2,0:T(4,128)} %param.11) | copy-start | bytes 49156
  1.5 14.1 %copy-start.41 = (f32[4,32,128]{2,1,0:T(8,128)S(1)}, f32[4,32,128]{2,1,0:T(8,128)}, u32[]{:S(2)}) copy-start(f32[4,32,128]{2,1,0:T(8,128)} %param.10) | copy-start | bytes 196612
  1.5 49.8 %copy-start.42 = (f32[4,32,128]{2,1,0:T(8,128)S(1)}, f32[4,32,128]{2,1,0:T(8,128)}, u32[]{:S(2)}) copy-start(f32[4,32,128]{2,1,0:T(8,128)} %param.9) | copy-start | bytes 196612
  2.8 56.5 %collective-permute-start = (f32[6,2,128,128]{3,2,1,0:T(8,128)}, f32[6,2,128,128]{3,2,1,0:T(8,128)S(1)}, u32[]{:S(2)}, u32[]{:S(2)}) collective-permute-start(f32[6,2,128,128]{3,2,1,0:T(8,128)} %get-tuple-element.47), channel_id=1, source_target_pairs={{4,0},{8,4},{12,8},{16,12},{20,16},{24,20},{28,24},{32,28},{36,32}... | collective-permute-start | bytes 2359304 | tf_op jit(solution)/shard_map/ppermute | solution.py:21
  5.5 53.8 %collective-permute-start.1 = (f32[6,2,128,128]{3,2,1,0:T(8,128)}, f32[6,2,128,128]{3,2,1,0:T(8,128)}, u32[]{:S(2)}, u32[]{:S(2)}) collective-permute-start(f32[6,2,128,128]{3,2,1,0:T(8,128)} %get-tuple-element.48), channel_id=1, source_target_pairs={{0,4},{4,8},{8,12},{12,16},{16,20},{20,24},{24,28},{28,32},{32,36}... | collective-permute-start | bytes 2359304 | tf_op jit(solution)/shard_map/ppermute | solution.py:20
  57.6 90.6 %copy-start.1 = (f32[4,128,128]{2,1,0:T(8,128)}, f32[4,128,128]{2,1,0:T(8,128)S(1)}, u32[]{:S(2)}) copy-start(f32[4,128,128]{2,1,0:T(8,128)S(1)} %multiply_exponential_fusion) | copy-start | bytes 786436
  57.6 2.2 copy-start
  57.7 90.5 %copy-start.5 = (f32[4,128,128]{2,1,0:T(8,128)}, f32[4,128,128]{2,1,0:T(8,128)S(1)}, u32[]{:S(2)}) copy-start(f32[4,128,128]{2,1,0:T(8,128)S(1)} %broadcast_multiply_fusion.1) | copy-start | bytes 786436
  61.2 87.1 %copy-start.8 = (f32[1,4,128,128]{3,2,1,0:T(8,128)}, f32[1,4,128,128]{3,2,1,0:T(8,128)S(1)}, u32[]{:S(2)}) copy-start(f32[1,4,128,128]{3,2,1,0:T(8,128)S(1)} %fusion.31) | copy-start | bytes 786436
  62.5 1.2 copy-start.11
  63.7 0.7 copy-start.15
  63.7 6.5 %copy-start.43 = (f32[4,32,128]{2,1,0:T(8,128)S(1)}, f32[4,32,128]{2,1,0:T(8,128)}, u32[]{:S(2)}) copy-start(f32[4,32,128]{2,1,0:T(8,128)} %param.8) | copy-start | bytes 196612
  63.9 22.3 %copy-start.44 = (f32[4,32,128]{2,1,0:T(8,128)S(1)}, f32[4,32,128]{2,1,0:T(8,128)}, u32[]{:S(2)}) copy-start(f32[4,32,128]{2,1,0:T(8,128)} %param.7) | copy-start | bytes 196612
  64.4 27.7 %collective-permute-start.2 = (f32[3,2,128,128]{3,2,1,0:T(8,128)S(1)}, f32[3,2,128,128]{3,2,1,0:T(8,128)S(1)}, u32[]{:S(2)}, u32[]{:S(2)}) collective-permute-start(f32[3,2,128,128]{3,2,1,0:T(8,128)S(1)} %get-tuple-element.67), channel_id=1, source_target_pairs={{0,4},{4,8},{8,12},{12,16},{16,20},{20,24},{24,28},{28,32},{32,36}... | collective-permute-start | bytes 1179656 | tf_op jit(solution)/shard_map/ppermute | solution.py:20
  66.3 25.8 %collective-permute-start.3 = (f32[3,2,128,128]{3,2,1,0:T(8,128)S(1)}, f32[3,2,128,128]{3,2,1,0:T(8,128)S(1)}, u32[]{:S(2)}, u32[]{:S(2)}) collective-permute-start(f32[3,2,128,128]{3,2,1,0:T(8,128)S(1)} %get-tuple-element.68), channel_id=1, source_target_pairs={{4,0},{8,4},{12,8},{16,12},{20,16},{24,20},{28,24},{32,28},{36,32}... | collective-permute-start | bytes 1179656 | tf_op jit(solution)/shard_map/ppermute | solution.py:21
  92.1 0.7 copy-start.19
  95.2 46.8 %collective-permute-start.4 = (f32[6,2,128,128]{3,2,1,0:T(8,128)}, f32[6,2,128,128]{3,2,1,0:T(8,128)S(1)}, u32[]{:S(2)}, u32[]{:S(2)}) collective-permute-start(f32[6,2,128,128]{3,2,1,0:T(8,128)} %get-tuple-element.45), channel_id=1, source_target_pairs={{4,0},{8,4},{12,8},{16,12},{20,16},{24,20},{28,24},{32,28},{36,32}... | collective-permute-start | bytes 2359304 | tf_op jit(solution)/shard_map/ppermute | solution.py:21
  97.1 47.2 %collective-permute-start.5 = (f32[6,2,128,128]{3,2,1,0:T(8,128)}, f32[6,2,128,128]{3,2,1,0:T(8,128)}, u32[]{:S(2)}, u32[]{:S(2)}) collective-permute-start(f32[6,2,128,128]{3,2,1,0:T(8,128)} %get-tuple-element.46), channel_id=1, source_target_pairs={{0,4},{4,8},{8,12},{12,16},{16,20},{20,24},{24,28},{28,32},{32,36}... | collective-permute-start | bytes 2359304 | tf_op jit(solution)/shard_map/ppermute | solution.py:20
  145.6 2.6 copy-start.23
  147.0 1.3 copy-start.26
  147.0 1.3 copy-start.12
  147.0 1.3 copy-start.16
  148.3 1.6 copy-start.29
  149.9 32.6 %copy-start.20 = (f32[4,128,128]{2,1,0:T(8,128)S(1)}, f32[4,128,128]{2,1,0:T(8,128)}, u32[]{:S(2)}) copy-start(f32[4,128,128]{2,1,0:T(8,128)} %copy-done.19) | copy-start | bytes 786436
  150.0 23.6 %collective-permute-start.6 = (f32[3,2,128,128]{3,2,1,0:T(8,128)S(1)}, f32[3,2,128,128]{3,2,1,0:T(8,128)S(1)}, u32[]{:S(2)}, u32[]{:S(2)}) collective-permute-start(f32[3,2,128,128]{3,2,1,0:T(8,128)S(1)} %get-tuple-element.62), channel_id=1, source_target_pairs={{0,4},{4,8},{8,12},{12,16},{16,20},{20,24},{24,28},{28,32},{32,36}... | collective-permute-start | bytes 1179656 | tf_op jit(solution)/shard_map/ppermute | solution.py:20
  160.7 21.8 %collective-permute-start.7 = (f32[3,2,128,128]{3,2,1,0:T(8,128)S(1)}, f32[3,2,128,128]{3,2,1,0:T(8,128)S(1)}, u32[]{:S(2)}, u32[]{:S(2)}) collective-permute-start(f32[3,2,128,128]{3,2,1,0:T(8,128)S(1)} %get-tuple-element.63), channel_id=1, source_target_pairs={{4,0},{8,4},{12,8},{16,12},{20,16},{24,20},{28,24},{32,28},{36,32}... | collective-permute-start | bytes 1179656 | tf_op jit(solution)/shard_map/ppermute | solution.py:21
  183.1 1.0 copy-start.2
  184.4 13.5 %copy-start.46 = (s32[1,64,4,4]{1,3,2,0:T(4,128)S(1)}, s32[1,64,4,4]{1,3,2,0:T(4,128)}, u32[]{:S(2)}) copy-start(s32[1,64,4,4]{1,3,2,0:T(4,128)} %get-tuple-element.69) | copy-start | bytes 12292
  184.4 13.5 %copy-start.47 = (s32[1,64,4,4]{1,3,2,0:T(4,128)S(1)}, s32[1,64,4,4]{1,3,2,0:T(4,128)}, u32[]{:S(2)}) copy-start(s32[1,64,4,4]{1,3,2,0:T(4,128)} %get-tuple-element.72) | copy-start | bytes 12292
  185.7 43.0 %collective-permute-start.8 = (f32[6,2,128,128]{3,2,1,0:T(8,128)}, f32[6,2,128,128]{3,2,1,0:T(8,128)S(1)}, u32[]{:S(2)}, u32[]{:S(2)}) collective-permute-start(f32[6,2,128,128]{3,2,1,0:T(8,128)} %get-tuple-element.38), channel_id=1, source_target_pairs={{4,0},{8,4},{12,8},{16,12},{20,16},{24,20},{28,24},{32,28},{36,32}... | collective-permute-start | bytes 2359304 | tf_op jit(solution)/shard_map/ppermute | solution.py:21
  187.6 42.3 %collective-permute-start.9 = (f32[6,2,128,128]{3,2,1,0:T(8,128)}, f32[6,2,128,128]{3,2,1,0:T(8,128)S(1)}, u32[]{:S(2)}, u32[]{:S(2)}) collective-permute-start(f32[6,2,128,128]{3,2,1,0:T(8,128)} %get-tuple-element.39), channel_id=1, source_target_pairs={{0,4},{4,8},{8,12},{12,16},{16,20},{20,24},{24,28},{28,32},{32,36}... | collective-permute-start | bytes 2359304 | tf_op jit(solution)/shard_map/ppermute | solution.py:20
  230.2 0.7 copy-start.32
  230.5 0.7 copy-start.34
  230.5 1.0 copy-start.3
  230.5 1.1 copy-start.6
  230.5 1.2 copy-start.9
  230.6 1.3 copy-start.13
  230.6 1.3 copy-start.17
  230.6 1.4 copy-start.24
  230.6 1.5 copy-start.27
  230.6 1.5 copy-start.30
  230.6 1.5 copy-start.38
  232.1 1.7 copy-start.36
  233.8 37.4 %copy-start.21 = (f32[4,128,128]{2,1,0:T(8,128)S(1)}, f32[4,128,128]{2,1,0:T(8,128)}, u32[]{:S(2)}) copy-start(f32[4,128,128]{2,1,0:T(8,128)} %copy-done.19) | copy-start | bytes 786436
  233.9 21.3 %collective-permute-start.10 = (f32[3,2,128,128]{3,2,1,0:T(8,128)S(1)}, f32[3,2,128,128]{3,2,1,0:T(8,128)S(1)}, u32[]{:S(2)}, u32[]{:S(2)}) collective-permute-start(f32[3,2,128,128]{3,2,1,0:T(8,128)S(1)} %get-tuple-element.57), channel_id=1, source_target_pairs={{0,4},{4,8},{8,12},{12,16},{16,20},{20,24},{24,28},{28,32},{32,36}... | collective-permute-start | bytes 1179656 | tf_op jit(solution)/shard_map/ppermute | solution.py:20
  244.6 26.6 %collective-permute-start.11 = (f32[3,2,128,128]{3,2,1,0:T(8,128)S(1)}, f32[3,2,128,128]{3,2,1,0:T(8,128)S(1)}, u32[]{:S(2)}, u32[]{:S(2)}) collective-permute-start(f32[3,2,128,128]{3,2,1,0:T(8,128)S(1)} %get-tuple-element.58), channel_id=1, source_target_pairs={{4,0},{8,4},{12,8},{16,12},{20,16},{24,20},{28,24},{32,28},{36,32}... | collective-permute-start | bytes 1179656 | tf_op jit(solution)/shard_map/ppermute | solution.py:21
  274.0 41.6 %collective-permute-start.12 = (f32[6,2,128,128]{3,2,1,0:T(8,128)}, f32[6,2,128,128]{3,2,1,0:T(8,128)S(1)}, u32[]{:S(2)}, u32[]{:S(2)}) collective-permute-start(f32[6,2,128,128]{3,2,1,0:T(8,128)} %get-tuple-element.31), channel_id=1, source_target_pairs={{4,0},{8,4},{12,8},{16,12},{20,16},{24,20},{28,24},{32,28},{36,32}... | collective-permute-start | bytes 2359304 | tf_op jit(solution)/shard_map/ppermute | solution.py:21
  275.9 39.9 %collective-permute-start.13 = (f32[6,2,128,128]{3,2,1,0:T(8,128)}, f32[6,2,128,128]{3,2,1,0:T(8,128)S(1)}, u32[]{:S(2)}, u32[]{:S(2)}) collective-permute-start(f32[6,2,128,128]{3,2,1,0:T(8,128)} %get-tuple-element.32), channel_id=1, source_target_pairs={{0,4},{4,8},{8,12},{12,16},{16,20},{20,24},{24,28},{28,32},{32,36}... | collective-permute-start | bytes 2359304 | tf_op jit(solution)/shard_map/ppermute | solution.py:20
  316.4 1.0 copy-start.4
  316.4 1.0 copy-start.7
  316.4 1.1 copy-start.10
  316.4 1.2 copy-start.14
  316.4 1.2 copy-start.18
  316.4 1.3 copy-start.25
  316.4 1.4 copy-start.28
  316.4 1.4 copy-start.31
  316.4 1.5 copy-start.33
  316.4 1.6 copy-start.35
  316.5 1.7 copy-start.37
  316.5 1.7 copy-start.39
  316.5 1.6 copy-start.40
  319.9 29.7 %copy-start.22 = (f32[4,128,128]{2,1,0:T(8,128)S(1)}, f32[4,128,128]{2,1,0:T(8,128)}, u32[]{:S(2)}) copy-start(f32[4,128,128]{2,1,0:T(8,128)} %copy-done.19) | copy-start | bytes 786436
  320.0 19.2 %collective-permute-start.14 = (f32[3,2,128,128]{3,2,1,0:T(8,128)S(1)}, f32[3,2,128,128]{3,2,1,0:T(8,128)S(1)}, u32[]{:S(2)}, u32[]{:S(2)}) collective-permute-start(f32[3,2,128,128]{3,2,1,0:T(8,128)S(1)} %get-tuple-element.52), channel_id=1, source_target_pairs={{0,4},{4,8},{8,12},{12,16},{16,20},{20,24},{24,28},{28,32},{32,36}... | collective-permute-start | bytes 1179656 | tf_op jit(solution)/shard_map/ppermute | solution.py:20
  330.6 19.0 %collective-permute-start.15 = (f32[3,2,128,128]{3,2,1,0:T(8,128)S(1)}, f32[3,2,128,128]{3,2,1,0:T(8,128)S(1)}, u32[]{:S(2)}, u32[]{:S(2)}) collective-permute-start(f32[3,2,128,128]{3,2,1,0:T(8,128)S(1)} %get-tuple-element.53), channel_id=1, source_target_pairs={{4,0},{8,4},{12,8},{16,12},{20,16},{24,20},{28,24},{32,28},{36,32}... | collective-permute-start | bytes 1179656 | tf_op jit(solution)/shard_map/ppermute | solution.py:21
where the time goes:
time: 354 us; the launch traced here: 353 us
  waiting for transfers between devices  146 us (41%)
  starting transfers between devices  94.9 us (27%)
  blocking collectives  63.3 us (18%)
  local copies, waits for them, and re-layouts  24.8 us (7%)
  other arithmetic  22.2 us (6%)
    ppermute x8, waiting for transfers between devices, extended(): after = lax.ppermute(initial, axis, down)  117 us
    ppermute x8, starting transfers between devices, extended(): before = lax.ppermute(last, axis, up)  76.6 us
    all_gather x1, blocking collectives, per_device(): lax.all_gather(quality, 'shot', axis=1, tiled=True)  35.7 us
    ppermute x8, waiting for transfers between devices, extended(): before = lax.ppermute(last, axis, up)  29.6 us
    ppermute x8, starting transfers between devices, extended(): after = lax.ppermute(initial, axis, down)  18.3 us
    all_gather x1, blocking collectives, per_device(): lax.all_gather(lame_mu, 'shot', axis=1, tiled=True)  15.9 us
    another operation x12, other arithmetic, velocity_update(): forcing = jnp.stack([grad_first, grad_second, grad_third])  9.36 us
    broadcast_in_dim x16, local copies, waits for them, and re-layouts, upsample(): return jnp.repeat(jnp.repeat(blocks, BLK, axis=1), BLK, axis=2)  9.27 us
  transfers between devices with their start and end apart: 16, of which 12 were waited for; matrix products, arithmetic and copies ran while one was open for 4% of the time, Pallas kernels for 0%

commit v1 on v0

--- a/solution.py
+++ b/solution.py
@@ -8,6 +8,16 @@
 COEF_NEAR = 1.125
 COEF_FAR = -1.0 / 24.0
 TIME_STEP = 0.2
+
+
+def list_area(inner_x, which_dim):
+    b_next = jnp.concatenate(
+        lax.all_to_all(
+            jnp.stack([inner_x for _ in range(lax.axis_size("shot"))], axis=0), "shot", 0, 0
+        ),
+        which_dim,
+    )
+    return b_next
 
 
 def extended(shard, sides, width):
@@ -118,7 +128,7 @@
         lax.all_gather(lame_lambda, "shot", axis=1, tiled=True),
         lax.all_gather(lame_mu, "shot", axis=1, tiled=True),
         lax.all_gather(buoyancy, "shot", axis=1, tiled=True),
-        lax.all_gather(quality, "shot", axis=1, tiled=True),
+        list_area(quality, 1),
     )
     model = jnp.stack(panels)
     values = wavefield[0]

time: 354 us -> 338 us (0.955); the launches traced: 353 us -> 333 us
  blocking collectives: 63.3 us -> 52.3 us
  waiting for transfers between devices: 146 us -> 137 us
    all_gather x1 -> x0, blocking collectives: 35.7 us -> none  [per_device(): lax.all_gather(quality, 'shot', axis=1, tiled=True)]
    all_gather x1, blocking collectives: 5.84 us -> 34 us  [per_device(): lax.all_gather(buoyancy, 'shot', axis=1, tiled=True)]
    ppermute x8, waiting for transfers between devices: 117 us -> 99.6 us  [extended(): after = lax.ppermute(initial, axis, down)]
    ppermute x8, waiting for transfers between devices: 29.6 us -> 37.3 us  [extended(): before = lax.ppermute(last, axis, up)]
    all_to_all x0 -> x1, starting transfers between devices: none -> 4.1 us  [list_area(): lax.all_to_all(jnp.stack([inner_x for _ in range(lax.axis_size('shot'))],...]
    another operation x12, other arithmetic: 9.36 us -> 5.43 us  [velocity_update(): forcing = jnp.stack([grad_first, grad_second, grad_third])]
    ppermute x8, starting transfers between devices: 76.6 us -> 72.7 us  [extended(): before = lax.ppermute(last, axis, up)]
  transfers between devices with their start and end apart: 16 -> 17, of which waited for: 12 -> 11; matrix products, arithmetic and copies ran while one was open for 4% -> 5% of each run, Pallas kernels for 0% -> 0%
where the time goes in v1:
time: 338 us; the launch traced here: 333 us
  waiting for transfers between devices  137 us (41%)
  starting transfers between devices  95.1 us (28%)
  blocking collectives  52.3 us (15%)
  local copies, waits for them, and re-layouts  27.4 us (8%)
  other arithmetic  20.1 us (6%)
    ppermute x8, waiting for transfers between devices, extended(): after = lax.ppermute(initial, axis, down)  99.6 us
    ppermute x8, starting transfers between devices, extended(): before = lax.ppermute(last, axis, up)  72.7 us
    ppermute x8, waiting for transfers between devices, extended(): before = lax.ppermute(last, axis, up)  37.3 us
    all_gather x1, blocking collectives, per_device(): lax.all_gather(buoyancy, 'shot', axis=1, tiled=True)  34 us
    ppermute x8, starting transfers between devices, extended(): after = lax.ppermute(initial, axis, down)  18.3 us
    all_gather x1, blocking collectives, per_device(): lax.all_gather(lame_mu, 'shot', axis=1, tiled=True)  12.4 us
    broadcast_in_dim x16, local copies, waits for them, and re-layouts, upsample(): return jnp.repeat(jnp.repeat(blocks, BLK, axis=1), BLK, axis=2)  9.32 us
  transfers between devices with their start and end apart: 17, of which 11 were waited for; matrix products, arithmetic and copies ran while one was open for 5% of the time, Pallas kernels for 0%

profile of v1, /device:TPU:126, one launch (start us, length us, event | category | flops | bytes accessed | tf_op | source)
XLA Modules:
  0.0 332.9 jit_solution(10323474194153710229)
XLA Ops:
  0.0 1.5 slice_bitcast_fusion
  1.5 1.2 fusion.437
  2.8 2.7 collective-permute-start
  5.5 9.4 %collective-permute-start.1 = (f32[6,2,128,128]{3,2,1,0:T(8,128)}, f32[6,2,128,128]{3,2,1,0:T(8,128)S(1)}, u32[]{:S(2)}, u32[]{:S(2)}) collective-permute-start(f32[6,2,128,128]{3,2,1,0:T(8,128)} %get-tuple-element.48), channel_id=1, source_target_pairs={{0,4},{4,8},{8,12},{12,16},{16,20},{20,24},{24,28},{28,32},{32,36}... | collective-permute-start | bytes 2359304 | tf_op jit(solution)/shard_map/ppermute | solution.py:30
  15.0 0.7 stack.139
  15.7 4.1 %all-to-all-start = ((f32[4,4,32,128]{3,2,1,0:T(8,128)}), f32[4,4,32,128]{3,2,1,0:T(8,128)}, u32[]{:S(2)}, u32[]{:S(2)}) async-start(f32[4,4,32,128]{3,2,1,0:T(8,128)} %stack.139), calls=%async_computation | async-start | bytes 524288 | tf_op jit(solution)/shard_map/all_to_all | solution.py:15
  19.8 0.6 fusion.442
  20.5 34.0 %all_gather.9 = f32[4,128,128]{2,1,0:T(8,128)} all-gather(f32[4,32,128]{2,1,0:T(8,128)S(1)} %copy-done.48), channel_id=1, replica_groups=mesh['aper'=64,'shot'=4] {'shot'}, dimensions={1}, use_global_device_ids=true | all-gather | bytes 327680 | tf_op jit(solution)/shard_map/all_gather | solution.py:130
  54.9 1.0 broadcast_multiply_fusion.1
  55.9 2.5 slice_bitcast_fusion.32
  58.4 1.0 fusion.381
  59.4 2.2 fusion.31
  62.2 0.6 copy-done.43
  63.6 0.4 copy-done.17
  64.0 1.9 collective-permute-start.2
  65.9 3.9 %collective-permute-start.3 = (f32[3,2,128,128]{3,2,1,0:T(8,128)S(1)}, f32[3,2,128,128]{3,2,1,0:T(8,128)S(1)}, u32[]{:S(2)}, u32[]{:S(2)}) collective-permute-start(f32[3,2,128,128]{3,2,1,0:T(8,128)S(1)} %get-tuple-element.68), channel_id=1, source_target_pairs={{4,0},{8,4},{12,8},{16,12},{20,16},{24,20},{28,24},{32,28},{36,32}... | collective-permute-start | bytes 1179656 | tf_op jit(solution)/shard_map/ppermute | solution.py:31
  69.8 12.4 %all_gather.11 = f32[4,128,128]{2,1,0:T(8,128)S(1)} all-gather(f32[4,32,128]{2,1,0:T(8,128)S(1)} %copy-done.49), channel_id=1, replica_groups=mesh['aper'=64,'shot'=4] {'shot'}, dimensions={1}, use_global_device_ids=true | all-gather | bytes 327680 | tf_op jit(solution)/shard_map/all_gather | solution.py:129
  82.3 5.8 %all_gather.10 = f32[4,128,128]{2,1,0:T(8,128)S(1)} all-gather(f32[4,32,128]{2,1,0:T(8,128)S(1)} %copy-done.50), channel_id=1, replica_groups=mesh['aper'=64,'shot'=4] {'shot'}, dimensions={1}, use_global_device_ids=true | all-gather | bytes 327680 | tf_op jit(solution)/shard_map/all_gather | solution.py:128
  90.0 1.2 fusion.436
  91.2 1.9 collective-permute-start.4
  93.2 13.1 %collective-permute-start.5 = (f32[6,2,128,128]{3,2,1,0:T(8,128)}, f32[6,2,128,128]{3,2,1,0:T(8,128)S(1)}, u32[]{:S(2)}, u32[]{:S(2)}) collective-permute-start(f32[6,2,128,128]{3,2,1,0:T(8,128)} %get-tuple-element.46), channel_id=1, source_target_pairs={{0,4},{4,8},{8,12},{12,16},{16,20},{20,24},{24,28},{28,32},{32,36}... | collective-permute-start | bytes 2359304 | tf_op jit(solution)/shard_map/ppermute | solution.py:30
  106.5 0.6 broadcast_in_dim.61
  107.1 0.9 copy.35
  108.2 30.9 %collective-permute-done.4 = f32[6,2,128,128]{3,2,1,0:T(8,128)S(1)} collective-permute-done((f32[6,2,128,128]{3,2,1,0:T(8,128)}, f32[6,2,128,128]{3,2,1,0:T(8,128)S(1)}, u32[]{:S(2)}, u32[]{:S(2)}) %collective-permute-start.4) | collective-permute-done | bytes 786464 | tf_op jit(solution)/shard_map/ppermute | solution.py:31
  139.1 1.6 collective-permute-done.5
  141.7 0.3 copy-done.28
  142.1 0.7 copy-done.31
  142.8 1.5 fusion.9
  144.4 10.7 %collective-permute-start.6 = (f32[3,2,128,128]{3,2,1,0:T(8,128)S(1)}, f32[3,2,128,128]{3,2,1,0:T(8,128)S(1)}, u32[]{:S(2)}, u32[]{:S(2)}) collective-permute-start(f32[3,2,128,128]{3,2,1,0:T(8,128)S(1)} %get-tuple-element.62), channel_id=1, source_target_pairs={{0,4},{4,8},{8,12},{12,16},{16,20},{20,24},{24,28},{28,32},{32,36}... | collective-permute-start | bytes 1179656 | tf_op jit(solution)/shard_map/ppermute | solution.py:30
  155.1 1.9 collective-permute-start.7
  157.1 13.1 %collective-permute-done.6 = f32[3,2,128,128]{3,2,1,0:T(8,128)S(1)} collective-permute-done((f32[3,2,128,128]{3,2,1,0:T(8,128)S(1)}, f32[3,2,128,128]{3,2,1,0:T(8,128)S(1)}, u32[]{:S(2)}, u32[]{:S(2)}) %collective-permute-start.6) | collective-permute-done | bytes 393248 | tf_op jit(solution)/shard_map/ppermute | solution.py:30
  170.2 14.3 %collective-permute-done.7 = f32[3,2,128,128]{3,2,1,0:T(8,128)S(1)} collective-permute-done((f32[3,2,128,128]{3,2,1,0:T(8,128)S(1)}, f32[3,2,128,128]{3,2,1,0:T(8,128)S(1)}, u32[]{:S(2)}, u32[]{:S(2)}) %collective-permute-start.7) | collective-permute-done | bytes 393248 | tf_op jit(solution)/shard_map/ppermute | solution.py:31
  185.7 0.3 multiply_add_fusion.2
  186.1 1.2 fusion.435
  187.3 1.9 collective-permute-start.8
  189.2 10.2 %collective-permute-start.9 = (f32[6,2,128,128]{3,2,1,0:T(8,128)}, f32[6,2,128,128]{3,2,1,0:T(8,128)S(1)}, u32[]{:S(2)}, u32[]{:S(2)}) collective-permute-start(f32[6,2,128,128]{3,2,1,0:T(8,128)} %get-tuple-element.39), channel_id=1, source_target_pairs={{0,4},{4,8},{8,12},{12,16},{16,20},{20,24},{24,28},{28,32},{32,36}... | collective-permute-start | bytes 2359304 | tf_op jit(solution)/shard_map/ppermute | solution.py:30
  199.6 0.7 copy.46
  200.3 0.8 broadcast_in_dim.63
  201.0 0.7 broadcast_in_dim.64
  201.7 1.3 broadcast_in_dim.65
  203.0 1.6 copy.38
  204.7 25.4 %collective-permute-done.8 = f32[6,2,128,128]{3,2,1,0:T(8,128)S(1)} collective-permute-done((f32[6,2,128,128]{3,2,1,0:T(8,128)}, f32[6,2,128,128]{3,2,1,0:T(8,128)S(1)}, u32[]{:S(2)}, u32[]{:S(2)}) %collective-permute-start.8) | collective-permute-done | bytes 786464 | tf_op jit(solution)/shard_map/ppermute | solution.py:31
  232.2 1.7 fusion.14
  234.0 6.5 %collective-permute-start.10 = (f32[3,2,128,128]{3,2,1,0:T(8,128)S(1)}, f32[3,2,128,128]{3,2,1,0:T(8,128)S(1)}, u32[]{:S(2)}, u32[]{:S(2)}) collective-permute-start(f32[3,2,128,128]{3,2,1,0:T(8,128)S(1)} %get-tuple-element.57), channel_id=1, source_target_pairs={{0,4},{4,8},{8,12},{12,16},{16,20},{20,24},{24,28},{28,32},{32,36}... | collective-permute-start | bytes 1179656 | tf_op jit(solution)/shard_map/ppermute | solution.py:30
  240.5 2.1 collective-permute-start.11
  242.7 7.1 %collective-permute-done.10 = f32[3,2,128,128]{3,2,1,0:T(8,128)S(1)} collective-permute-done((f32[3,2,128,128]{3,2,1,0:T(8,128)S(1)}, f32[3,2,128,128]{3,2,1,0:T(8,128)S(1)}, u32[]{:S(2)}, u32[]{:S(2)}) %collective-permute-start.10) | collective-permute-done | bytes 393248 | tf_op jit(solution)/shard_map/ppermute | solution.py:30
  249.7 6.8 %collective-permute-done.11 = f32[3,2,128,128]{3,2,1,0:T(8,128)S(1)} collective-permute-done((f32[3,2,128,128]{3,2,1,0:T(8,128)S(1)}, f32[3,2,128,128]{3,2,1,0:T(8,128)S(1)}, u32[]{:S(2)}, u32[]{:S(2)}) %collective-permute-start.11) | collective-permute-done | bytes 393248 | tf_op jit(solution)/shard_map/ppermute | solution.py:31
  257.7 0.3 multiply_add_fusion.1
  258.0 1.2 fusion.434
  259.3 1.9 collective-permute-start.12
  261.2 10.2 %collective-permute-start.13 = (f32[6,2,128,128]{3,2,1,0:T(8,128)}, f32[6,2,128,128]{3,2,1,0:T(8,128)S(1)}, u32[]{:S(2)}, u32[]{:S(2)}) collective-permute-start(f32[6,2,128,128]{3,2,1,0:T(8,128)} %get-tuple-element.32), channel_id=1, source_target_pairs={{0,4},{4,8},{8,12},{12,16},{16,20},{20,24},{24,28},{28,32},{32,36}... | collective-permute-start | bytes 2359304 | tf_op jit(solution)/shard_map/ppermute | solution.py:30
  271.4 0.7 copy.47
  272.1 0.7 broadcast_in_dim.67
  272.9 0.6 broadcast_in_dim.69
  273.6 1.6 copy.41
  275.3 14.1 %collective-permute-done.12 = f32[6,2,128,128]{3,2,1,0:T(8,128)S(1)} collective-permute-done((f32[6,2,128,128]{3,2,1,0:T(8,128)}, f32[6,2,128,128]{3,2,1,0:T(8,128)S(1)}, u32[]{:S(2)}, u32[]{:S(2)}) %collective-permute-start.12) | collective-permute-done | bytes 786464 | tf_op jit(solution)/shard_map/ppermute | solution.py:31
  289.3 9.6 %collective-permute-done.13 = f32[6,2,128,128]{3,2,1,0:T(8,128)S(1)} collective-permute-done((f32[6,2,128,128]{3,2,1,0:T(8,128)}, f32[6,2,128,128]{3,2,1,0:T(8,128)S(1)}, u32[]{:S(2)}, u32[]{:S(2)}) %collective-permute-start.13) | collective-permute-done | bytes 786464 | tf_op jit(solution)/shard_map/ppermute | solution.py:30
  299.9 0.5 copy-done.4
  301.3 1.8 fusion.19
  303.1 10.6 %collective-permute-start.14 = (f32[3,2,128,128]{3,2,1,0:T(8,128)S(1)}, f32[3,2,128,128]{3,2,1,0:T(8,128)S(1)}, u32[]{:S(2)}, u32[]{:S(2)}) collective-permute-start(f32[3,2,128,128]{3,2,1,0:T(8,128)S(1)} %get-tuple-element.52), channel_id=1, source_target_pairs={{0,4},{4,8},{8,12},{12,16},{16,20},{20,24},{24,28},{28,32},{32,36}... | collective-permute-start | bytes 1179656 | tf_op jit(solution)/shard_map/ppermute | solution.py:30
  313.7 1.9 collective-permute-start.15
  315.7 5.9 %collective-permute-done.14 = f32[3,2,128,128]{3,2,1,0:T(8,128)S(1)} collective-permute-done((f32[3,2,128,128]{3,2,1,0:T(8,128)S(1)}, f32[3,2,128,128]{3,2,1,0:T(8,128)S(1)}, u32[]{:S(2)}, u32[]{:S(2)}) %collective-permute-start.14) | collective-permute-done | bytes 393248 | tf_op jit(solution)/shard_map/ppermute | solution.py:30
  321.6 8.2 %collective-permute-done.15 = f32[3,2,128,128]{3,2,1,0:T(8,128)S(1)} collective-permute-done((f32[3,2,128,128]{3,2,1,0:T(8,128)S(1)}, f32[3,2,128,128]{3,2,1,0:T(8,128)S(1)}, u32[]{:S(2)}, u32[]{:S(2)}) %collective-permute-start.15) | collective-permute-done | bytes 393248 | tf_op jit(solution)/shard_map/ppermute | solution.py:31
  331.3 1.6 maximum_bitcast_fusion
  (169 shorter events, 13.1 us)
Async XLA Ops:
  1.5 13.5 %copy-start.47 = (f32[4,32,128]{2,1,0:T(8,128)S(1)}, f32[4,32,128]{2,1,0:T(8,128)}, u32[]{:S(2)}) copy-start(f32[4,32,128]{2,1,0:T(8,128)} %param.10) | copy-start | bytes 196612
  1.5 18.3 %copy-start.51 = (s32[4,64,4,4]{1,3,2,0:T(4,128)S(1)}, s32[4,64,4,4]{1,3,2,0:T(4,128)}, u32[]{:S(2)}) copy-start(s32[4,64,4,4]{1,3,2,0:T(4,128)} %param.11) | copy-start | bytes 49156
  1.5 19.0 %copy-start.48 = (f32[4,32,128]{2,1,0:T(8,128)S(1)}, f32[4,32,128]{2,1,0:T(8,128)}, u32[]{:S(2)}) copy-start(f32[4,32,128]{2,1,0:T(8,128)} %param.9) | copy-start | bytes 196612
  2.8 56.6 %collective-permute-start = (f32[6,2,128,128]{3,2,1,0:T(8,128)}, f32[6,2,128,128]{3,2,1,0:T(8,128)S(1)}, u32[]{:S(2)}, u32[]{:S(2)}) collective-permute-start(f32[6,2,128,128]{3,2,1,0:T(8,128)} %get-tuple-element.47), channel_id=1, source_target_pairs={{4,0},{8,4},{12,8},{16,12},{20,16},{24,20},{28,24},{32,28},{36,32}... | collective-permute-start | bytes 2359304 | tf_op jit(solution)/shard_map/ppermute | solution.py:31
  5.5 53.9 %collective-permute-start.1 = (f32[6,2,128,128]{3,2,1,0:T(8,128)}, f32[6,2,128,128]{3,2,1,0:T(8,128)S(1)}, u32[]{:S(2)}, u32[]{:S(2)}) collective-permute-start(f32[6,2,128,128]{3,2,1,0:T(8,128)} %get-tuple-element.48), channel_id=1, source_target_pairs={{0,4},{4,8},{8,12},{12,16},{16,20},{20,24},{24,28},{28,32},{32,36}... | collective-permute-start | bytes 2359304 | tf_op jit(solution)/shard_map/ppermute | solution.py:30
  15.7 42.7 %all-to-all-start = ((f32[4,4,32,128]{3,2,1,0:T(8,128)}), f32[4,4,32,128]{3,2,1,0:T(8,128)}, u32[]{:S(2)}, u32[]{:S(2)}) async-start(f32[4,4,32,128]{3,2,1,0:T(8,128)} %stack.139), calls=%async_computation | async-start | bytes 524288 | tf_op jit(solution)/shard_map/all_to_all | solution.py:15
  55.9 7.4 %copy-start.5 = (f32[4,128,128]{2,1,0:T(8,128)}, f32[4,128,128]{2,1,0:T(8,128)S(1)}, u32[]{:S(2)}) copy-start(f32[4,128,128]{2,1,0:T(8,128)S(1)} %broadcast_multiply_fusion.1) | copy-start | bytes 786436
  59.4 30.3 %copy-start.1 = (f32[4,4,32,128]{3,2,0,1:T(8,128)}, f32[4,4,32,128]{3,2,0,1:T(8,128)S(1)}, u32[]{:S(2)}) copy-start(f32[4,4,32,128]{3,2,0,1:T(8,128)S(1)} %fusion.381) | copy-start | bytes 786436
  59.4 2.5 copy-start
  59.4 2.4 copy-start.34
  59.4 2.5 copy-start.45
  61.6 1.6 copy-start.9
  61.9 0.9 copy-start.43
  61.9 1.0 copy-start.44
  62.2 1.1 copy-start.13
  63.3 6.5 %copy-start.49 = (f32[4,32,128]{2,1,0:T(8,128)S(1)}, f32[4,32,128]{2,1,0:T(8,128)}, u32[]{:S(2)}) copy-start(f32[4,32,128]{2,1,0:T(8,128)} %param.8) | copy-start | bytes 196612
  63.5 18.8 %copy-start.50 = (f32[4,32,128]{2,1,0:T(8,128)S(1)}, f32[4,32,128]{2,1,0:T(8,128)}, u32[]{:S(2)}) copy-start(f32[4,32,128]{2,1,0:T(8,128)} %param.7) | copy-start | bytes 196612
  64.0 24.2 %collective-permute-start.2 = (f32[3,2,128,128]{3,2,1,0:T(8,128)S(1)}, f32[3,2,128,128]{3,2,1,0:T(8,128)S(1)}, u32[]{:S(2)}, u32[]{:S(2)}) collective-permute-start(f32[3,2,128,128]{3,2,1,0:T(8,128)S(1)} %get-tuple-element.67), channel_id=1, source_target_pairs={{0,4},{4,8},{8,12},{12,16},{16,20},{20,24},{24,28},{28,32},{32,36}... | collective-permute-start | bytes 1179656 | tf_op jit(solution)/shard_map/ppermute | solution.py:30
  65.9 22.3 %collective-permute-start.3 = (f32[3,2,128,128]{3,2,1,0:T(8,128)S(1)}, f32[3,2,128,128]{3,2,1,0:T(8,128)S(1)}, u32[]{:S(2)}, u32[]{:S(2)}) collective-permute-start(f32[3,2,128,128]{3,2,1,0:T(8,128)S(1)} %get-tuple-element.68), channel_id=1, source_target_pairs={{4,0},{8,4},{12,8},{16,12},{20,16},{24,20},{28,24},{32,28},{36,32}... | collective-permute-start | bytes 1179656 | tf_op jit(solution)/shard_map/ppermute | solution.py:31
  91.2 47.8 %collective-permute-start.4 = (f32[6,2,128,128]{3,2,1,0:T(8,128)}, f32[6,2,128,128]{3,2,1,0:T(8,128)S(1)}, u32[]{:S(2)}, u32[]{:S(2)}) collective-permute-start(f32[6,2,128,128]{3,2,1,0:T(8,128)} %get-tuple-element.45), channel_id=1, source_target_pairs={{4,0},{8,4},{12,8},{16,12},{20,16},{24,20},{28,24},{32,28},{36,32}... | collective-permute-start | bytes 2359304 | tf_op jit(solution)/shard_map/ppermute | solution.py:31
  93.2 47.6 %collective-permute-start.5 = (f32[6,2,128,128]{3,2,1,0:T(8,128)}, f32[6,2,128,128]{3,2,1,0:T(8,128)S(1)}, u32[]{:S(2)}, u32[]{:S(2)}) collective-permute-start(f32[6,2,128,128]{3,2,1,0:T(8,128)} %get-tuple-element.46), channel_id=1, source_target_pairs={{0,4},{4,8},{8,12},{12,16},{16,20},{20,24},{24,28},{28,32},{32,36}... | collective-permute-start | bytes 2359304 | tf_op jit(solution)/shard_map/ppermute | solution.py:30
  141.3 1.4 copy-start.2
  141.4 1.4 copy-start.6
  141.4 1.4 copy-start.10
  141.4 1.4 copy-start.14
  141.4 1.4 copy-start.18
  144.3 40.2 %copy-start.22 = (f32[4,128,128]{2,1,0:T(8,128)S(1)}, f32[4,128,128]{2,1,0:T(8,128)}, u32[]{:S(2)}) copy-start(f32[4,128,128]{2,1,0:T(8,128)} %copy-done.21) | copy-start | bytes 786436
  144.4 25.8 %collective-permute-start.6 = (f32[3,2,128,128]{3,2,1,0:T(8,128)S(1)}, f32[3,2,128,128]{3,2,1,0:T(8,128)S(1)}, u32[]{:S(2)}, u32[]{:S(2)}) collective-permute-start(f32[3,2,128,128]{3,2,1,0:T(8,128)S(1)} %get-tuple-element.62), channel_id=1, source_target_pairs={{0,4},{4,8},{8,12},{12,16},{16,20},{20,24},{24,28},{28,32},{32,36}... | collective-permute-start | bytes 1179656 | tf_op jit(solution)/shard_map/ppermute | solution.py:30
  155.1 29.5 %collective-permute-start.7 = (f32[3,2,128,128]{3,2,1,0:T(8,128)S(1)}, f32[3,2,128,128]{3,2,1,0:T(8,128)S(1)}, u32[]{:S(2)}, u32[]{:S(2)}) collective-permute-start(f32[3,2,128,128]{3,2,1,0:T(8,128)S(1)} %get-tuple-element.63), channel_id=1, source_target_pairs={{4,0},{8,4},{12,8},{16,12},{20,16},{24,20},{28,24},{32,28},{36,32}... | collective-permute-start | bytes 1179656 | tf_op jit(solution)/shard_map/ppermute | solution.py:31
  186.0 13.4 %copy-start.52 = (s32[1,64,4,4]{1,3,2,0:T(4,128)S(1)}, s32[1,64,4,4]{1,3,2,0:T(4,128)}, u32[]{:S(2)}) copy-start(s32[1,64,4,4]{1,3,2,0:T(4,128)} %get-tuple-element.69) | copy-start | bytes 12292
  186.0 13.4 %copy-start.53 = (s32[1,64,4,4]{1,3,2,0:T(4,128)S(1)}, s32[1,64,4,4]{1,3,2,0:T(4,128)}, u32[]{:S(2)}) copy-start(s32[1,64,4,4]{1,3,2,0:T(4,128)} %get-tuple-element.72) | copy-start | bytes 12292
  187.3 42.7 %collective-permute-start.8 = (f32[6,2,128,128]{3,2,1,0:T(8,128)}, f32[6,2,128,128]{3,2,1,0:T(8,128)S(1)}, u32[]{:S(2)}, u32[]{:S(2)}) collective-permute-start(f32[6,2,128,128]{3,2,1,0:T(8,128)} %get-tuple-element.38), channel_id=1, source_target_pairs={{4,0},{8,4},{12,8},{16,12},{20,16},{24,20},{28,24},{32,28},{36,32}... | collective-permute-start | bytes 2359304 | tf_op jit(solution)/shard_map/ppermute | solution.py:31
  189.2 40.8 %collective-permute-start.9 = (f32[6,2,128,128]{3,2,1,0:T(8,128)}, f32[6,2,128,128]{3,2,1,0:T(8,128)S(1)}, u32[]{:S(2)}, u32[]{:S(2)}) collective-permute-start(f32[6,2,128,128]{3,2,1,0:T(8,128)} %get-tuple-element.39), channel_id=1, source_target_pairs={{0,4},{4,8},{8,12},{12,16},{16,20},{20,24},{24,28},{28,32},{32,36}... | collective-permute-start | bytes 2359304 | tf_op jit(solution)/shard_map/ppermute | solution.py:30
  230.6 1.0 copy-start.3
  230.6 1.1 copy-start.7
  230.6 1.2 copy-start.11
  230.7 1.3 copy-start.15
  230.7 1.3 copy-start.19
  230.7 1.4 copy-start.26
  230.7 1.5 copy-start.29
  230.7 1.5 copy-start.32
  230.7 1.5 copy-start.41
  232.2 1.7 copy-start.39
  233.9 22.6 %copy-start.23 = (f32[4,128,128]{2,1,0:T(8,128)S(1)}, f32[4,128,128]{2,1,0:T(8,128)}, u32[]{:S(2)}) copy-start(f32[4,128,128]{2,1,0:T(8,128)} %copy-done.21) | copy-start | bytes 786436
  234.0 15.7 %collective-permute-start.10 = (f32[3,2,128,128]{3,2,1,0:T(8,128)S(1)}, f32[3,2,128,128]{3,2,1,0:T(8,128)S(1)}, u32[]{:S(2)}, u32[]{:S(2)}) collective-permute-start(f32[3,2,128,128]{3,2,1,0:T(8,128)S(1)} %get-tuple-element.57), channel_id=1, source_target_pairs={{0,4},{4,8},{8,12},{12,16},{16,20},{20,24},{24,28},{28,32},{32,36}... | collective-permute-start | bytes 1179656 | tf_op jit(solution)/shard_map/ppermute | solution.py:30
  240.5 16.0 %collective-permute-start.11 = (f32[3,2,128,128]{3,2,1,0:T(8,128)S(1)}, f32[3,2,128,128]{3,2,1,0:T(8,128)S(1)}, u32[]{:S(2)}, u32[]{:S(2)}) collective-permute-start(f32[3,2,128,128]{3,2,1,0:T(8,128)S(1)} %get-tuple-element.58), channel_id=1, source_target_pairs={{4,0},{8,4},{12,8},{16,12},{20,16},{24,20},{28,24},{32,28},{36,32}... | collective-permute-start | bytes 1179656 | tf_op jit(solution)/shard_map/ppermute | solution.py:31
  259.3 30.1 %collective-permute-start.12 = (f32[6,2,128,128]{3,2,1,0:T(8,128)}, f32[6,2,128,128]{3,2,1,0:T(8,128)S(1)}, u32[]{:S(2)}, u32[]{:S(2)}) collective-permute-start(f32[6,2,128,128]{3,2,1,0:T(8,128)} %get-tuple-element.31), channel_id=1, source_target_pairs={{4,0},{8,4},{12,8},{16,12},{20,16},{24,20},{28,24},{32,28},{36,32}... | collective-permute-start | bytes 2359304 | tf_op jit(solution)/shard_map/ppermute | solution.py:31
  261.2 37.7 %collective-permute-start.13 = (f32[6,2,128,128]{3,2,1,0:T(8,128)}, f32[6,2,128,128]{3,2,1,0:T(8,128)S(1)}, u32[]{:S(2)}, u32[]{:S(2)}) collective-permute-start(f32[6,2,128,128]{3,2,1,0:T(8,128)} %get-tuple-element.32), channel_id=1, source_target_pairs={{0,4},{4,8},{8,12},{12,16},{16,20},{20,24},{24,28},{28,32},{32,36}... | collective-permute-start | bytes 2359304 | tf_op jit(solution)/shard_map/ppermute | solution.py:30
  299.5 1.0 copy-start.4
  299.5 1.0 copy-start.8
  299.5 1.1 copy-start.12
  299.5 1.2 copy-start.16
  299.5 1.2 copy-start.20
  299.5 1.3 copy-start.27
  299.5 1.4 copy-start.30
  299.6 1.4 copy-start.33
  299.6 1.5 copy-start.36
  299.6 1.6 copy-start.38
  299.6 1.7 copy-start.40
  299.6 1.7 copy-start.42
  299.6 1.6 copy-start.46
  303.0 26.8 %copy-start.24 = (f32[4,128,128]{2,1,0:T(8,128)S(1)}, f32[4,128,128]{2,1,0:T(8,128)}, u32[]{:S(2)}) copy-start(f32[4,128,128]{2,1,0:T(8,128)} %copy-done.21) | copy-start | bytes 786436
  303.1 18.5 %collective-permute-start.14 = (f32[3,2,128,128]{3,2,1,0:T(8,128)S(1)}, f32[3,2,128,128]{3,2,1,0:T(8,128)S(1)}, u32[]{:S(2)}, u32[]{:S(2)}) collective-permute-start(f32[3,2,128,128]{3,2,1,0:T(8,128)S(1)} %get-tuple-element.52), channel_id=1, source_target_pairs={{0,4},{4,8},{8,12},{12,16},{16,20},{20,24},{24,28},{28,32},{32,36}... | collective-permute-start | bytes 1179656 | tf_op jit(solution)/shard_map/ppermute | solution.py:30
  313.7 16.1 %collective-permute-start.15 = (f32[3,2,128,128]{3,2,1,0:T(8,128)S(1)}, f32[3,2,128,128]{3,2,1,0:T(8,128)S(1)}, u32[]{:S(2)}, u32[]{:S(2)}) collective-permute-start(f32[3,2,128,128]{3,2,1,0:T(8,128)S(1)} %get-tuple-element.53), channel_id=1, source_target_pairs={{4,0},{8,4},{12,8},{16,12},{20,16},{24,20},{28,24},{32,28},{36,32}... | collective-permute-start | bytes 1179656 | tf_op jit(solution)/shard_map/ppermute | solution.py:31
  (7 other events, 5.0 us)
